TPU v7x, 32 devices: a whole 2x2x4 slice. The times are simulated.
32 devices in a mesh: groups: 2 (over y), replica: 16 (over z, x, core).
Axes of the slice: x: 2, y: 2, z: 4, core: 2. Of those that a mesh axis runs over, the one named last changes fastest.
Arguments:
- queries: bfloat16 [64, 4, 4096], P(('groups', 'replica')), parts along dimension 0, may hold values from -4 to 4
- keys: bfloat16 [64, 4, 4096], P(('groups', 'replica')), parts along dimension 0, may hold values from -4 to 4
- values: bfloat16 [64, 4, 4096], P(('groups', 'replica')), parts along dimension 0, may hold values from -6 to 6
- gate_input: bfloat16 [64, 4, 4096], P(('groups', 'replica')), parts along dimension 0, may hold values from -6 to 6
- decay_rate: float32 [32], replicated, may hold values from 0.05 to 1.5
- norm_gain: float32 [4096], replicated, may hold values from 0.1 to 1.9
- out_weight: bfloat16 [4096, 3072], P('replica'), may hold values from -0.09375 to 0.09375
- prompt_states: bfloat16 [8, 4096, 128], P('groups', 'replica'), parts along dimension 0, may hold values from -4 to 4
- group_sizes: int32 [8], P('groups'), parts along dimension 0, may hold values from 1 to 16, 32 in all
Outputs:
- mixed: bfloat16 [64, 4, 3072], P(('groups', 'replica')), parts along dimension 0
There are 2 independent parts, one for each index of `groups`. A program takes and returns all parts, laid end to end along the dimension named above; an argument that names none is the same for every part. Nothing has to cross between parts.
Inputs may be any that keep to these rules, and one draw needn't show every extreme that they name: `group_sizes`: the group sizes sum to 32, and the largest is exactly 16.
All inputs are finite; a program needn't handle non-finite values.
Results may differ from a plain program's by a relative error of at most 0.005.
Values may be sent and summed in bfloat16 or wider, within the bound.
No kernel may reach another device: no remote copies, remote signals or barrier semaphores. Data moves between devices by JAX's collectives and lax.ppermute only.
A program may use at most 64 MiB of HBM per device.

v0:
```python
import jax
import jax.numpy as jnp
from jax import lax
from jax.sharding import PartitionSpec as P


def on_device(
    queries, keys, values, gate_input, decay_rate, norm_gain, out_weight, prompt_states, group_sizes
):
    replicas = lax.axis_size("replica")
    rows_local, steps_count, features = queries.shape
    head_size = prompt_states.shape[2]
    head_count = features // head_size
    share = prompt_states.shape[1]
    rows_total = rows_local * replicas
    ends = jnp.cumsum(group_sizes)
    row_ids = jnp.arange(rows_total, dtype=jnp.int32)
    owners = jnp.sum((row_ids[:, None] >= ends[None, :]).astype(jnp.int32), axis=1)
    q_four = queries.reshape(rows_local, steps_count, head_count, head_size)
    k_four = keys.reshape(rows_local, steps_count, head_count, head_size)
    v_four = values.astype(jnp.float32).reshape(rows_local, steps_count, head_count, head_size)
    piece = min(share, head_size)
    pieces_here = share // piece
    per_head = head_size // piece
    query_parts = queries.reshape(rows_local, steps_count, replicas, share)
    held_queries = lax.all_to_all(query_parts, "replica", split_axis=2, concat_axis=0, tiled=True)
    held_queries = held_queries.reshape(rows_total, steps_count, pieces_here, piece)
    held_states = jnp.take(prompt_states, owners, axis=0).reshape(
        rows_total, pieces_here, piece, head_size
    )
    partial_value = jnp.einsum(
        "rtcd,rcde->rtce", held_queries, held_states, preferred_element_type=jnp.float32
    )
    partial_value = partial_value.reshape(replicas, rows_local, steps_count, pieces_here, head_size)
    returned = lax.all_to_all(partial_value, "replica", split_axis=0, concat_axis=0, tiled=True)
    returned = jnp.moveaxis(returned, 0, 2)
    returned = returned.reshape(rows_local, steps_count, head_count, per_head, head_size)
    prompt_read = jnp.sum(returned, axis=3)
    times = jnp.arange(1, steps_count + 1).astype(jnp.float32)
    lead = jnp.exp(-times[:, None] * decay_rate[None, :])
    gap = times[:, None] - times[None, :]
    weights_mix = jnp.where(
        gap[None] >= 0.0, jnp.exp(-jnp.maximum(gap, 0.0)[None] * decay_rate[:, None, None]), 0.0
    )
    scores = jnp.einsum("rthd,rshd->rhts", q_four, k_four, preferred_element_type=jnp.float32)
    recent = jnp.einsum(
        "rhts,rshe->rthe", scores * weights_mix[None], v_four, precision=lax.Precision.HIGHEST
    )
    attention = lead[None, :, :, None] * prompt_read + recent
    attention = attention.reshape(rows_local, steps_count, features)
    mean_square = jnp.mean(attention * attention, axis=-1, keepdims=True)
    gate = jax.nn.sigmoid(gate_input.astype(jnp.float32))
    hidden = (attention * lax.rsqrt(mean_square + 1e-06) * norm_gain * gate).astype(jnp.bfloat16)
    hidden = hidden.reshape(rows_local * steps_count, features)
    columns_held = lax.all_to_all(hidden, "replica", split_axis=1, concat_axis=0, tiled=True)
    mixed = lax.psum_scatter(
        jnp.dot(columns_held, out_weight, preferred_element_type=jnp.float32),
        "replica",
        scatter_dimension=0,
        tiled=True,
    )
    return mixed.astype(jnp.bfloat16).reshape(rows_local, steps_count, out_weight.shape[1])


def solution(mesh):
    in_specs = (
        P(("groups", "replica"), None, None),
        P(("groups", "replica"), None, None),
        P(("groups", "replica"), None, None),
        P(("groups", "replica"), None, None),
        P(),
        P(),
        P("replica", None),
        P("groups", "replica", None),
        P("groups"),
    )
    out_specs = P(("groups", "replica"), None, None)
    return jax.shard_map(
        on_device, mesh=mesh, in_specs=in_specs, out_specs=out_specs, check_vma=False
    )
```

profile of v0, /device:TPU:0, one launch (start us, length us, event | category | flops | bytes accessed | tf_op | source)
XLA Modules:
  0.0 114.7 jit_solution(6417857061044807749)
XLA Ops:
  6.5 0.0 copy-start
  6.5 1.6 %copy.47 = bf16[2,1,16,4,256]{4,3,1,0,2:T(4,128)(2,1)} copy(bf16[2,1,16,4,256]{4,3,2,1,0:T(4,128)(2,1)} %bitcast.54) | data formatting | bytes 131072 | tf_op jit(solution)/shard_map/reshape | solution.py:25
  8.1 7.4 %all-to-all-start = ((bf16[2,4,16,256]{3,1,0,2:T(4,128)(2,1)}), bf16[2,4,16,256]{3,1,0,2:T(4,128)(2,1)S(1)}, u32[]{:S(2)}, u32[]{:S(2)}) async-start(bf16[2,4,16,256]{3,1,0,2:T(4,128)(2,1)} %bitcast.51), calls=%async_computation | async-start | bytes 131072 | tf_op jit(solution)/shard_map/all_to_all | solution.py:26
  15.5 0.8 reduce-window.8
  16.4 0.1 convert_reduce_fusion
  16.5 0.1 fusion.12
  16.5 0.1 subtract_compare_fusion
  16.6 0.8 exponential_select_fusion
  17.4 3.1 %gather_fusion = bf16[32,256,128]{2,1,0:T(8,128)(2,1)} fusion(bf16[4,256,128]{2,1,0:T(8,128)(2,1)} %param.16, s32[1024]{0:T(1024)S(1)} %pad_clamp_fusion), kind=kCustom, calls=%fused_computation | custom fusion | bytes 4194432 | tf_op jit(solution)/shard_map/jit(_take)/gather | solution.py:28
  20.5 1.9 %all-to-all-done = bf16[2,4,16,256]{3,1,0,2:T(4,128)(2,1)S(1)} async-done(((bf16[2,4,16,256]{3,1,0,2:T(4,128)(2,1)}), bf16[2,4,16,256]{3,1,0,2:T(4,128)(2,1)S(1)}, u32[]{:S(2)}, u32[]{:S(2)}) %all-to-all-start) | async-done | bytes 65568 | tf_op jit(solution)/shard_map/all_to_all | solution.py:26
  22.4 0.0 copy-start.5
  22.4 0.0 copy-start.1
  22.4 0.0 copy-start.2
  22.4 0.0 copy-start.6
  22.4 0.0 copy-start.3
  22.4 0.0 copy-start.4
  22.5 3.0 %fusion = f32[32,2,128,4]{2,3,1,0:T(4,128)} fusion(bf16[32,4,2,128]{3,1,2,0:T(4,128)(2,1)S(1)} %bitcast.56, bf16[32,2,128,128]{3,2,1,0:T(8,128)(2,1)} %bitcast.52, pred[32]{0:T(512)(128)(4,1)S(1)} %compare_and_fusion), kind=kOutput, calls=%fused_computation.1 | convolution fusion | flops 9437184 | bytes 2293792 | tf_op jit(solution)/shard_map/rtcd,rcde->rtce/dot_general | solution.py:31
  25.5 4.1 %all-to-all-start.1 = ((f32[16,2,4,2,128]{4,2,3,1,0:T(4,128)}), f32[16,2,4,2,128]{4,2,3,1,0:T(4,128)S(1)}, u32[]{:S(2)}, u32[]{:S(2)}) async-start(f32[16,2,4,2,128]{4,2,3,1,0:T(4,128)} %bitcast.9), calls=%async_computation.1 | async-start | bytes 262144 | tf_op jit(solution)/shard_map/all_to_all | solution.py:35
  29.6 0.0 reduce-scatter.2.cloned.1.call-start
  29.7 0.0 copy-done.5
  29.7 0.1 multiply_exponential_fusion
  29.8 0.1 copy.37
  29.9 0.0 copy-done.1
  29.9 0.0 copy-done.2
  29.9 0.2 convolution_multiply_fusion
  30.1 7.5 %all-to-all-done.1 = f32[16,2,4,2,128]{4,2,3,1,0:T(4,128)S(1)} async-done(((f32[16,2,4,2,128]{4,2,3,1,0:T(4,128)}), f32[16,2,4,2,128]{4,2,3,1,0:T(4,128)S(1)}, u32[]{:S(2)}, u32[]{:S(2)}) %all-to-all-start.1) | async-done | bytes 131104 | tf_op jit(solution)/shard_map/all_to_all | solution.py:35
  37.6 0.0 copy-done.6
  37.6 0.4 multiply_reduce_fusion
  38.0 0.0 copy-done.3
  38.0 0.0 copy-done.4
  38.0 0.1 fusion.6
  38.2 9.5 %all_to_all.39 = bf16[8,16,256]{2,0,1:T(8,128)(2,1)S(1)} all-to-all(bf16[8,16,256]{2,0,1:T(8,128)(2,1)S(1)} %copy.44), channel_id=1, replica_groups=mesh['groups'=2,'replica'=16] {'replica'}, dimensions={1} | all-to-all | bytes 131072 | tf_op jit(solution)/shard_map/all_to_all | solution.py:55
  47.7 0.0 copy-done
  47.7 1.6 %fusion.7 = f32[128,3072]{1,0:T(8,128)} fusion(bf16[256,3072]{1,0:T(8,128)(2,1)S(1)} %copy-done, bf16[8,16,256]{2,0,1:T(8,128)(2,1)S(1)} %all_to_all.39), kind=kOutput, calls=%fused_computation.14 | convolution fusion | flops 201326592 | bytes 3211264 | tf_op jit(solution)/shard_map/dot_general | solution.py:57
  49.2 0.0 reduce-scatter.2.cloned.1.call-update
  49.3 57.0 %reduce-scatter.2.cloned.1.call-done = f32[8,3072]{1,0:T(8,128)} async-done(((f32[128,3072]{1,0:T(8,128)}), f32[8,3072]{1,0:T(8,128)}) %reduce-scatter.2.cloned.1.call-update) | async-done | bytes 98320 | tf_op jit(solution)/shard_map/reduce_scatter | solution.py:56
  106.3 0.9 convert_element_type.35
  107.2 0.6 reshape.202
  (9 shorter events, 0.1 us)
Async XLA Ops:
  6.5 41.2 %copy-start = (bf16[256,3072]{1,0:T(8,128)(2,1)S(1)}, bf16[256,3072]{1,0:T(8,128)(2,1)}, u32[]{:S(2)}) copy-start(bf16[256,3072]{1,0:T(8,128)(2,1)} %param.15) | copy-start | bytes 4718596
  8.1 14.3 %all-to-all-start = ((bf16[2,4,16,256]{3,1,0,2:T(4,128)(2,1)}), bf16[2,4,16,256]{3,1,0,2:T(4,128)(2,1)S(1)}, u32[]{:S(2)}, u32[]{:S(2)}) async-start(bf16[2,4,16,256]{3,1,0,2:T(4,128)(2,1)} %bitcast.51), calls=%async_computation | async-start | bytes 131072 | tf_op jit(solution)/shard_map/all_to_all | solution.py:26
  22.4 7.3 %copy-start.5 = (f32[32]{0:T(128)S(1)}, f32[32]{0:T(128)}, u32[]{:S(2)}) copy-start(f32[32]{0:T(128)} %param.13) | copy-start | bytes 388
  22.4 7.4 %copy-start.1 = (bf16[2,4,4096]{2,1,0:T(4,128)(2,1)S(1)}, bf16[2,4,4096]{2,1,0:T(4,128)(2,1)}, u32[]{:S(2)}) copy-start(bf16[2,4,4096]{2,1,0:T(4,128)(2,1)} %param.9) | copy-start | bytes 196612
  22.4 7.4 %copy-start.2 = (bf16[2,4,4096]{2,1,0:T(4,128)(2,1)S(1)}, bf16[2,4,4096]{2,1,0:T(4,128)(2,1)}, u32[]{:S(2)}) copy-start(bf16[2,4,4096]{2,1,0:T(4,128)(2,1)} %param.10) | copy-start | bytes 196612
  22.4 15.1 %copy-start.6 = (bf16[2,4,4096]{2,1,0:T(4,128)(2,1)S(1)}, bf16[2,4,4096]{2,1,0:T(4,128)(2,1)}, u32[]{:S(2)}) copy-start(bf16[2,4,4096]{2,1,0:T(4,128)(2,1)} %param.11) | copy-start | bytes 196612
  22.4 15.6 %copy-start.3 = (bf16[2,4,4096]{2,1,0:T(4,128)(2,1)S(1)}, bf16[2,4,4096]{2,1,0:T(4,128)(2,1)}, u32[]{:S(2)}) copy-start(bf16[2,4,4096]{2,1,0:T(4,128)(2,1)} %param.12) | copy-start | bytes 196612
  22.4 15.6 %copy-start.4 = (f32[4096]{0:T(1024)S(1)}, f32[4096]{0:T(1024)}, u32[]{:S(2)}) copy-start(f32[4096]{0:T(1024)} %param.14) | copy-start | bytes 49156
  25.5 12.1 %all-to-all-start.1 = ((f32[16,2,4,2,128]{4,2,3,1,0:T(4,128)}), f32[16,2,4,2,128]{4,2,3,1,0:T(4,128)S(1)}, u32[]{:S(2)}, u32[]{:S(2)}) async-start(f32[16,2,4,2,128]{4,2,3,1,0:T(4,128)} %bitcast.9), calls=%async_computation.1 | async-start | bytes 262144 | tf_op jit(solution)/shard_map/all_to_all | solution.py:35
  29.6 76.6 %reduce-scatter.2.cloned.1.call-start = ((), (), s32[]{:S(2)}) async-start(), calls=%async_computation.4 | async-start | bytes 1671168 | tf_op jit(solution)/shard_map/reduce_scatter | solution.py:56
Sparse Core Ops, SparseCore 0:
  49.4 56.8 reduce-scatter.1
where the time goes:
time: 115 us
  waiting for transfers between devices  66.4 us (58%)
  between operations  13.5 us (12%)
  starting transfers between devices  11.6 us (10%)
  blocking collectives  9.48 us (8%)
  local copies, waits for them, and re-layouts  5.53 us (5%)
  matrix products  5.23 us (5%)
  other arithmetic  2.95 us (3%)
    reduce_scatter x1, waiting for transfers between devices, on_device(): lax.psum_scatter(jnp.dot(columns_held, out_weight, preferred_element_type...  57 us
    all_to_all x1, blocking collectives, on_device(): lax.all_to_all(hidden, 'replica', split_axis=1, concat_axis=0, tiled=True)  9.48 us
    all_to_all x1, waiting for transfers between devices, on_device(): lax.all_to_all(partial_value, 'replica', split_axis=0, concat_axis=0, til...  7.46 us
    all_to_all x1, starting transfers between devices, on_device(): lax.all_to_all(query_parts, 'replica', split_axis=2, concat_axis=0, tiled...  7.39 us
    all_to_all x1, starting transfers between devices, on_device(): lax.all_to_all(partial_value, 'replica', split_axis=0, concat_axis=0, til...  4.14 us
    gather x1, local copies, waits for them, and re-layouts, on_device(): jnp.take(prompt_states, owners, axis=0)  3.1 us
    dot_general x1, matrix products, on_device(): jnp.einsum('rtcd,rcde->rtce', held_queries, held_states, preferred_elemen...  3.02 us
  transfers between devices with their start and end apart: 3, of which 3 were waited for; matrix products, arithmetic and copies ran while one was open for 5% of the time, Pallas kernels for 0%

commit v1 on v0

--- a/solution.py
+++ b/solution.py
@@ -1,10 +1,18 @@
+import functools
+
 import jax
 import jax.numpy as jnp
 from jax import lax
+from jax.experimental import pallas as pl
+from jax.experimental.pallas import tpu as pltpu
 from jax.sharding import PartitionSpec as P
 
-
-def on_device(
+LANES = 128
+EPSILON = 1e-06
+CORES = 2
+
+
+def partial_plan(
     queries, keys, values, gate_input, decay_rate, norm_gain, out_weight, prompt_states, group_sizes
 ):
     replicas = lax.axis_size("replica")
@@ -50,7 +58,7 @@
     attention = attention.reshape(rows_local, steps_count, features)
     mean_square = jnp.mean(attention * attention, axis=-1, keepdims=True)
     gate = jax.nn.sigmoid(gate_input.astype(jnp.float32))
-    hidden = (attention * lax.rsqrt(mean_square + 1e-06) * norm_gain * gate).astype(jnp.bfloat16)
+    hidden = (attention * lax.rsqrt(mean_square + EPSILON) * norm_gain * gate).astype(jnp.bfloat16)
     hidden = hidden.reshape(rows_local * steps_count, features)
     columns_held = lax.all_to_all(hidden, "replica", split_axis=1, concat_axis=0, tiled=True)
     mixed = lax.psum_scatter(
@@ -62,6 +70,185 @@
     return mixed.astype(jnp.bfloat16).reshape(rows_local, steps_count, out_weight.shape[1])
 
 
+def pack_kernel(q_ref, k_ref, v_ref, g_ref, send_ref):
+    chips, _, _, width = send_ref.shape
+    rows, steps, _ = q_ref.shape
+    for array, ref in enumerate((q_ref, k_ref, v_ref, g_ref)):
+        for chip in range(chips):
+            window = slice(chip * width, (chip + 1) * width)
+            for row in range(rows):
+                send_ref[chip, array, row * steps : (row + 1) * steps, :] = ref[row, :, window]
+
+
+def head_kernel(
+    rows, steps, rate_ref, size_ref, recv_ref, gain_ref, own_state, other_state, own_weight,
+    other_weight, part_ref, hidden_ref, weight_ref, sems,
+):
+    chips, _, per_chip, _ = recv_ref.shape
+    count = chips * per_chip
+    prompts, share, head = own_state.shape
+    heads_here = share // head
+    device = lax.axis_index("replica")
+    chip = device // CORES
+    core = lax.rem(device, CORES)
+    copies = [
+        pltpu.make_async_copy(source, weight_ref.at[slot * share : (slot + 1) * share], sems.at[slot])
+        for slot, source in enumerate((own_weight, other_weight))
+    ]
+    for copy in copies:
+        copy.start()
+    index = lax.broadcasted_iota(jnp.int32, (count, head), 0)
+    row = (index // per_chip * CORES + core) * rows + index % per_chip // steps
+    time = (index % steps + 1).astype(jnp.float32)
+    here = []
+    first = jnp.int32(0)
+    for prompt in range(prompts):
+        last = first + size_ref[prompt]
+        here.append((row >= first) & (row < last))
+        first = last
+    left = lax.broadcasted_iota(jnp.int32, (count, count), 0)
+    right = lax.broadcasted_iota(jnp.int32, (count, count), 1)
+    joined = (left // steps == right // steps) & (left >= right)
+    gap = jnp.maximum(left - right, 0).astype(jnp.float32)
+    squares = jnp.zeros((count, head), jnp.float32)
+    for slot, state in enumerate((own_state, other_state)):
+        place = core if slot == 0 else CORES - 1 - core
+        for part in range(heads_here):
+            number = (chip * CORES + place) * heads_here + part
+            rate = rate_ref[number]
+            window = pl.ds(pl.multiple_of(place * share + part * head, head), head)
+            query, key, value, gate = (
+                recv_ref[:, array, :, window].astype(jnp.float32).reshape(count, head)
+                for array in range(4)
+            )
+            held = slice(part * head, (part + 1) * head)
+            read = jnp.zeros((count, head), jnp.float32)
+            for prompt in range(prompts):
+                picked = jnp.where(here[prompt], query, 0.0).astype(jnp.bfloat16)
+                read += jnp.dot(picked, state[prompt, held, :], preferred_element_type=jnp.float32)
+            scores = lax.dot_general(
+                query.astype(jnp.bfloat16),
+                key.astype(jnp.bfloat16),
+                (((1,), (1,)), ((), ())),
+                preferred_element_type=jnp.float32,
+            )
+            scores = jnp.where(joined, scores * jnp.exp(-gap * rate), 0.0)
+            high = scores.astype(jnp.bfloat16)
+            rest = scores - high.astype(jnp.float32)
+            low = rest.astype(jnp.bfloat16)
+            value = value.astype(jnp.bfloat16)
+            recent = jnp.dot(high, value, preferred_element_type=jnp.float32)
+            recent += jnp.dot(low, value, preferred_element_type=jnp.float32)
+            attention = jnp.exp(-time * rate) * read + recent
+            squares += attention * attention
+            scaled = attention * gain_ref[pl.ds(number, 1), :] * jax.nn.sigmoid(gate)
+            column = slot * share + part * head
+            hidden_ref[:, column : column + head] = scaled.astype(jnp.bfloat16)
+    total = jnp.sum(squares, axis=1, keepdims=True)
+    high = total.astype(jnp.bfloat16).astype(jnp.float32)
+    middle = (total - high).astype(jnp.bfloat16).astype(jnp.float32)
+    low = total - high - middle
+    lane = lax.broadcasted_iota(jnp.int32, (count, LANES), 1)
+    tail = jnp.where(lane == 0, high, jnp.where(lane == 1, middle, jnp.where(lane == 2, low, 0.0)))
+    width = own_weight.shape[1]
+    part_ref[:, :, width:] = tail.reshape(chips, per_chip, LANES).astype(part_ref.dtype)
+    for copy in copies:
+        copy.wait()
+    tile = 512 if width % 512 == 0 else LANES
+    for start in range(0, width, tile):
+        columns = slice(start, start + tile)
+        block = jnp.dot(hidden_ref[...], weight_ref[:, columns], preferred_element_type=jnp.float32)
+        part_ref[:, :, columns] = block.reshape(chips, per_chip, tile).astype(part_ref.dtype)
+
+
+def finish_kernel(features, part_ref, mixed_ref):
+    rows, steps, width = mixed_ref.shape
+    tail = jnp.sum(part_ref[:, :, width:].astype(jnp.float32), axis=0)
+    squares = jnp.sum(tail, axis=1, keepdims=True)
+    scale = lax.rsqrt(squares / features + EPSILON)
+    tile = 512 if width % 512 == 0 else LANES
+    for start in range(0, width, tile):
+        columns = slice(start, start + tile)
+        block = jnp.sum(part_ref[:, :, columns].astype(jnp.float32), axis=0) * scale
+        mixed_ref[:, :, columns] = block.reshape(rows, steps, tile).astype(mixed_ref.dtype)
+
+
+def whole_plan(
+    queries, keys, values, gate_input, decay_rate, norm_gain, out_weight, prompt_states, group_sizes
+):
+    replicas = lax.axis_size("replica")
+    rows, steps, features = queries.shape
+    prompts, share, head = prompt_states.shape
+    width = out_weight.shape[1]
+    chips = replicas // CORES
+    per_chip = rows * steps
+    wide = share * CORES
+    swap = [(i, i + 1 - 2 * (i % CORES)) for i in range(replicas)]
+    peers = [[i * CORES + core for i in range(chips)] for core in range(CORES)]
+    other_state = lax.ppermute(prompt_states, "replica", swap)
+    other_weight = lax.ppermute(out_weight, "replica", swap)
+    vmem = pl.BlockSpec(memory_space=pltpu.VMEM)
+    smem = pl.BlockSpec(memory_space=pltpu.SMEM)
+    whole = pl.BlockSpec(memory_space=pl.ANY)
+    limit = pltpu.CompilerParams(vmem_limit_bytes=24 << 20)
+    sent = pl.pallas_call(
+        pack_kernel,
+        out_shape=jax.ShapeDtypeStruct((chips, 4, per_chip, wide), queries.dtype),
+        in_specs=[vmem] * 4,
+        out_specs=vmem,
+        compiler_params=limit,
+        name="pack",
+    )(queries, keys, values, gate_input)
+    exchange = functools.partial(
+        lax.all_to_all,
+        axis_name="replica",
+        split_axis=0,
+        concat_axis=0,
+        tiled=True,
+        axis_index_groups=peers,
+    )
+    held = exchange(sent)
+    parts = pl.pallas_call(
+        functools.partial(head_kernel, rows, steps),
+        out_shape=jax.ShapeDtypeStruct((chips, per_chip, width + LANES), jnp.bfloat16),
+        in_specs=[smem, smem, vmem, vmem, vmem, vmem, whole, whole],
+        out_specs=vmem,
+        scratch_shapes=[
+            pltpu.VMEM((chips * per_chip, wide), jnp.bfloat16),
+            pltpu.VMEM((wide, width), out_weight.dtype),
+            pltpu.SemaphoreType.DMA((2,)),
+        ],
+        compiler_params=limit,
+        name="heads",
+    )(
+        decay_rate,
+        group_sizes,
+        held,
+        norm_gain.reshape(features // head, head),
+        prompt_states,
+        other_state,
+        out_weight,
+        other_weight,
+    )
+    returned = exchange(parts)
+    return pl.pallas_call(
+        functools.partial(finish_kernel, features),
+        out_shape=jax.ShapeDtypeStruct((rows, steps, width), jnp.bfloat16),
+        in_specs=[vmem],
+        out_specs=vmem,
+        compiler_params=limit,
+        name="finish",
+    )(returned)
+
+
+def on_device(*arguments):
+    states = arguments[7]
+    replicas = lax.axis_size("replica")
+    if states.shape[1] % states.shape[2] == 0 and replicas % CORES == 0:
+        return whole_plan(*arguments)
+    return partial_plan(*arguments)
+
+
 def solution(mesh):
     in_specs = (
         P(("groups", "replica"), None, None),

time: 115 us -> 44.7 us (0.39)
  waiting for transfers between devices: 66.4 us -> 9.36 us
  between operations: 13.5 us -> 0.02 us
  blocking collectives: 9.48 us -> 15.9 us
  matrix products: 5.23 us -> 0 us
  starting transfers between devices: 11.6 us -> 7.51 us
  Pallas kernels: 0 us -> 3.61 us
  other arithmetic: 2.95 us -> 0 us
  local copies, waits for them, and re-layouts: 5.53 us -> 7.74 us
    reduce_scatter x1 -> x0, waiting for transfers between devices: 57 us -> none  [on_device(): lax.psum_scatter(jnp.dot(columns_held, out_weight, preferred_element_type...]
    unnamed x14 -> x18, local copies, waits for them, and re-layouts: 0.03 us -> 7.74 us
    all_to_all x1, blocking collectives: 9.48 us -> 15.9 us  [whole_plan(): returned = exchange(parts)]
    dot_general x4 -> x0, matrix products: 5.23 us -> none  [the longest x1 3.02 us: on_device(): jnp.einsum('rtcd,rcde->rtce', held_queries, held_states, preferred_elemen...]
    all_to_all x2 -> x1, starting transfers between devices: 11.5 us -> 6.79 us  [whole_plan(): held = exchange(sent)]
    pallas_call x0 -> x3, Pallas kernels: none -> 3.61 us  [the longest x1 2.11 us: whole_plan(): pl.pallas_call(functools.partial(head_kernel, rows, steps), out_shape=jax...]
    gather x1 -> x0, local copies, waits for them, and re-layouts: 3.1 us -> none  [on_device(): jnp.take(prompt_states, owners, axis=0)]
    reshape x2 -> x0, local copies, waits for them, and re-layouts: 2.24 us -> none  [the longest x1 1.59 us: on_device(): query_parts = queries.reshape(rows_local, steps_count, replicas, share)]
  transfers between devices with their start and end apart: 3 -> 3, of which waited for: 3 -> 2; matrix products, arithmetic and copies ran while one was open for 5% -> 0% of each run, Pallas kernels for 0% -> 2%
where the time goes in v1:
time: 44.7 us; the launch traced here: 44.2 us
  blocking collectives  15.9 us (36%)
  waiting for transfers between devices  9.36 us (21%)
  local copies, waits for them, and re-layouts  7.74 us (17%)
  starting transfers between devices  7.51 us (17%)
  Pallas kernels  3.61 us (8%)
    all_to_all x1, blocking collectives, whole_plan(): returned = exchange(parts)  15.9 us
    all_to_all x1, waiting for transfers between devices, whole_plan(): held = exchange(sent)  7.84 us
    unnamed x18, local copies, waits for them, and re-layouts  7.74 us
    all_to_all x1, starting transfers between devices, whole_plan(): held = exchange(sent)  6.79 us
    pallas_call x1, Pallas kernels, whole_plan(): pl.pallas_call(functools.partial(head_kernel, rows, steps), out_shape=jax...  2.11 us
    ppermute x1, waiting for transfers between devices, whole_plan(): other_state = lax.ppermute(prompt_states, 'replica', swap)  1.52 us
  transfers between devices with their start and end apart: 3, of which 2 were waited for; matrix products, arithmetic and copies ran while one was open for 0% of the time, Pallas kernels for 2%

profile of v1, /device:TPU:0, one launch (start us, length us, event | category | flops | bytes accessed | tf_op | source)
XLA Modules:
  0.0 44.2 jit_solution(12828741081244813189)
XLA Ops:
  0.0 0.5 %collective-permute-start.1 = (bf16[256,3072]{1,0:T(8,128)(2,1)}, bf16[256,3072]{1,0:T(8,128)(2,1)S(1)}, u32[]{:S(2)}, u32[]{:S(2)}) collective-permute-start(bf16[256,3072]{1,0:T(8,128)(2,1)} %own_weight.1), channel_id=1, source_target_pairs={{0,1},{1,0},{2,3},{3,2},{4,5},{5,4},{6,7},{7,6},{8,9},{9,8},{10,11... | collective-permute-start | bytes 4718600 | tf_op jit(solution)/shard_map/ppermute | solution.py:189
  0.5 0.0 copy-start.2
  0.5 0.8 %copy-done.2 = bf16[2,4,4096]{2,1,0:T(4,128)(2,1)S(1)} copy-done((bf16[2,4,4096]{2,1,0:T(4,128)(2,1)S(1)}, bf16[2,4,4096]{2,1,0:T(4,128)(2,1)}, u32[]{:S(2)}) %copy-start.2) | copy-done | bytes 65560
  1.3 0.0 copy-start.3
  1.3 0.8 %copy-done.3 = bf16[2,4,4096]{2,1,0:T(4,128)(2,1)S(1)} copy-done((bf16[2,4,4096]{2,1,0:T(4,128)(2,1)S(1)}, bf16[2,4,4096]{2,1,0:T(4,128)(2,1)}, u32[]{:S(2)}) %copy-start.3) | copy-done | bytes 65560
  2.2 0.0 copy-start.4
  2.2 0.8 %copy-done.4 = bf16[2,4,4096]{2,1,0:T(4,128)(2,1)S(1)} copy-done((bf16[2,4,4096]{2,1,0:T(4,128)(2,1)S(1)}, bf16[2,4,4096]{2,1,0:T(4,128)(2,1)}, u32[]{:S(2)}) %copy-start.4) | copy-done | bytes 65560
  3.0 0.0 copy-start.5
  3.0 0.8 %copy-done.5 = bf16[2,4,4096]{2,1,0:T(4,128)(2,1)S(1)} copy-done((bf16[2,4,4096]{2,1,0:T(4,128)(2,1)S(1)}, bf16[2,4,4096]{2,1,0:T(4,128)(2,1)}, u32[]{:S(2)}) %copy-start.5) | copy-done | bytes 65560
  3.9 0.8 %pack.1 = bf16[8,4,8,512]{3,2,1,0:T(8,128)(2,1)} custom-call(bf16[2,4,4096]{2,1,0:T(4,128)(2,1)S(1)} %copy-done.2, bf16[2,4,4096]{2,1,0:T(4,128)(2,1)S(1)} %copy-done.3, bf16[2,4,4096]{2,1,0:T(4,128)(2,1)S(1)} %copy-done.4, bf16[2,4,4096]{2,1,0:T(4,128)(2,1)S(1)} %copy-done.5), custom_call_target="tpu_custom_call" | custom-call | tf_op jit(solution)/shard_map/pack/pallas_call | solution.py:194
  4.6 6.8 %all-to-all-start = ((bf16[8,4,8,512]{3,2,1,0:T(8,128)(2,1)}), bf16[8,4,8,512]{3,2,1,0:T(8,128)(2,1)S(1)}, u32[]{:S(2)}, u32[]{:S(2)}) async-start(bf16[8,4,8,512]{3,2,1,0:T(8,128)(2,1)} %pack.1), calls=%async_computation | async-start | bytes 524288 | tf_op jit(solution)/shard_map/all_to_all | solution.py:210
  11.4 0.2 collective-permute-start
  11.6 1.5 %collective-permute-done.other_state = bf16[4,256,128]{2,1,0:T(8,128)(2,1)S(1)} collective-permute-done((bf16[4,256,128]{2,1,0:T(8,128)(2,1)}, bf16[4,256,128]{2,1,0:T(8,128)(2,1)S(1)}, u32[]{:S(2)}, u32[]{:S(2)}) %collective-permute-start) | collective-permute-done | bytes 262176 | tf_op jit(solution)/shard_map/ppermute | solution.py:188
  13.2 7.8 %all-to-all-done.recv_ref = bf16[8,4,8,512]{3,2,1,0:T(8,128)(2,1)S(1)} async-done(((bf16[8,4,8,512]{3,2,1,0:T(8,128)(2,1)}), bf16[8,4,8,512]{3,2,1,0:T(8,128)(2,1)S(1)}, u32[]{:S(2)}, u32[]{:S(2)}) %all-to-all-start) | async-done | bytes 262176 | tf_op jit(solution)/shard_map/all_to_all | solution.py:210
  21.0 0.0 collective-permute-done.1.other_weight
  21.0 0.0 copy-start
  21.0 1.4 %copy-done = bf16[256,3072]{1,0:T(8,128)(2,1)S(1)} copy-done((bf16[256,3072]{1,0:T(8,128)(2,1)S(1)}, bf16[256,3072]{1,0:T(8,128)(2,1)}, u32[]{:S(2)}) %copy-start) | copy-done | bytes 1572888
  22.4 0.0 copy-start.1
  22.4 0.9 %copy-done.1 = bf16[4,256,128]{2,1,0:T(8,128)(2,1)S(1)} copy-done((bf16[4,256,128]{2,1,0:T(8,128)(2,1)S(1)}, bf16[4,256,128]{2,1,0:T(8,128)(2,1)}, u32[]{:S(2)}) %copy-start.1) | copy-done | bytes 262168
  23.4 0.0 copy-start.6
  23.4 0.7 %copy-done.6 = f32[4096]{0:T(1024)S(1)} copy-done((f32[4096]{0:T(1024)S(1)}, f32[4096]{0:T(1024)}, u32[]{:S(2)}) %copy-start.6) | copy-done | bytes 16408
  24.1 0.0 copy-start.7
  24.1 0.7 %copy-done.7 = f32[32]{0:T(128)S(1)} copy-done((f32[32]{0:T(128)S(1)}, f32[32]{0:T(128)}, u32[]{:S(2)}) %copy-start.7) | copy-done | bytes 152
  24.7 0.0 copy-start.8
  24.7 0.7 %copy-done.8 = s32[4]{0:T(128)S(1)} copy-done((s32[4]{0:T(128)S(1)}, s32[4]{0:T(128)}, u32[]{:S(2)}) %copy-start.8) | copy-done | bytes 40
  25.4 2.1 %heads.1 = bf16[8,8,3200]{2,1,0:T(8,128)(2,1)S(1)} custom-call(f32[32]{0:T(128)S(1)} %copy-done.7, s32[4]{0:T(128)S(1)} %copy-done.8, bf16[8,4,8,512]{3,2,1,0:T(8,128)(2,1)S(1)} %all-to-all-done.recv_ref, f32[32,128]{1,0:T(8,128)S(1)} %bitcast.1, bf16[4,256,128]{2,1,0:T(8,128)(2,1)S(1)} %copy-done.1, ...), custom_call_target="tpu_custom_call" | custom-call | tf_op jit(solution)/shard_map/heads/pallas_call | solution.py:211
  27.5 15.9 %all_to_all.10.part_ref = bf16[8,8,3200]{2,1,0:T(8,128)(2,1)S(1)} all-to-all(bf16[8,8,3200]{2,1,0:T(8,128)(2,1)S(1)} %heads.1), channel_id=1, replica_groups={{0,2,4,6,8,10,12,14},{1,3,5,7,9,11,13,15},{16,18,20,22,24,26,28,30},{17..., dimensions={0} | all-to-all | bytes 819200 | tf_op jit(solution)/shard_map/all_to_all | solution.py:233
  43.4 0.7 %finish.1 = bf16[2,4,3072]{2,1,0:T(4,128)(2,1)} custom-call(bf16[8,8,3200]{2,1,0:T(8,128)(2,1)S(1)} %all_to_all.10.part_ref), custom_call_target="tpu_custom_call" | custom-call | tf_op jit(solution)/shard_map/finish/pallas_call | solution.py:234
Async XLA Ops:
  0.0 21.0 %collective-permute-start.1 = (bf16[256,3072]{1,0:T(8,128)(2,1)}, bf16[256,3072]{1,0:T(8,128)(2,1)S(1)}, u32[]{:S(2)}, u32[]{:S(2)}) collective-permute-start(bf16[256,3072]{1,0:T(8,128)(2,1)} %own_weight.1), channel_id=1, source_target_pairs={{0,1},{1,0},{2,3},{3,2},{4,5},{5,4},{6,7},{7,6},{8,9},{9,8},{10,11... | collective-permute-start | bytes 4718600 | tf_op jit(solution)/shard_map/ppermute | solution.py:189
  0.5 0.8 %copy-start.2 = (bf16[2,4,4096]{2,1,0:T(4,128)(2,1)S(1)}, bf16[2,4,4096]{2,1,0:T(4,128)(2,1)}, u32[]{:S(2)}) copy-start(bf16[2,4,4096]{2,1,0:T(4,128)(2,1)} %q_ref.1) | copy-start | bytes 196612
  1.3 0.8 %copy-start.3 = (bf16[2,4,4096]{2,1,0:T(4,128)(2,1)S(1)}, bf16[2,4,4096]{2,1,0:T(4,128)(2,1)}, u32[]{:S(2)}) copy-start(bf16[2,4,4096]{2,1,0:T(4,128)(2,1)} %k_ref.1) | copy-start | bytes 196612
  2.2 0.8 %copy-start.4 = (bf16[2,4,4096]{2,1,0:T(4,128)(2,1)S(1)}, bf16[2,4,4096]{2,1,0:T(4,128)(2,1)}, u32[]{:S(2)}) copy-start(bf16[2,4,4096]{2,1,0:T(4,128)(2,1)} %v_ref.1) | copy-start | bytes 196612
  3.0 0.8 %copy-start.5 = (bf16[2,4,4096]{2,1,0:T(4,128)(2,1)S(1)}, bf16[2,4,4096]{2,1,0:T(4,128)(2,1)}, u32[]{:S(2)}) copy-start(bf16[2,4,4096]{2,1,0:T(4,128)(2,1)} %g_ref.1) | copy-start | bytes 196612
  4.6 16.4 %all-to-all-start = ((bf16[8,4,8,512]{3,2,1,0:T(8,128)(2,1)}), bf16[8,4,8,512]{3,2,1,0:T(8,128)(2,1)S(1)}, u32[]{:S(2)}, u32[]{:S(2)}) async-start(bf16[8,4,8,512]{3,2,1,0:T(8,128)(2,1)} %pack.1), calls=%async_computation | async-start | bytes 524288 | tf_op jit(solution)/shard_map/all_to_all | solution.py:210
  11.4 1.7 %collective-permute-start = (bf16[4,256,128]{2,1,0:T(8,128)(2,1)}, bf16[4,256,128]{2,1,0:T(8,128)(2,1)S(1)}, u32[]{:S(2)}, u32[]{:S(2)}) collective-permute-start(bf16[4,256,128]{2,1,0:T(8,128)(2,1)} %own_state.1), channel_id=1, source_target_pairs={{0,1},{1,0},{2,3},{3,2},{4,5},{5,4},{6,7},{7,6},{8,9},{9,8},{10,11... | collective-permute-start | bytes 786440 | tf_op jit(solution)/shard_map/ppermute | solution.py:188
  21.0 1.4 %copy-start = (bf16[256,3072]{1,0:T(8,128)(2,1)S(1)}, bf16[256,3072]{1,0:T(8,128)(2,1)}, u32[]{:S(2)}) copy-start(bf16[256,3072]{1,0:T(8,128)(2,1)} %own_weight.1) | copy-start | bytes 4718596
  22.4 0.9 %copy-start.1 = (bf16[4,256,128]{2,1,0:T(8,128)(2,1)S(1)}, bf16[4,256,128]{2,1,0:T(8,128)(2,1)}, u32[]{:S(2)}) copy-start(bf16[4,256,128]{2,1,0:T(8,128)(2,1)} %own_state.1) | copy-start | bytes 786436
  23.4 0.7 %copy-start.6 = (f32[4096]{0:T(1024)S(1)}, f32[4096]{0:T(1024)}, u32[]{:S(2)}) copy-start(f32[4096]{0:T(1024)} %param.14) | copy-start | bytes 49156
  24.1 0.7 %copy-start.7 = (f32[32]{0:T(128)S(1)}, f32[32]{0:T(128)}, u32[]{:S(2)}) copy-start(f32[32]{0:T(128)} %rate_ref.1) | copy-start | bytes 388
  24.7 0.7 %copy-start.8 = (s32[4]{0:T(128)S(1)}, s32[4]{0:T(128)}, u32[]{:S(2)}) copy-start(s32[4]{0:T(128)} %size_ref.1) | copy-start | bytes 52

commit v2 on v1

--- a/solution.py
+++ b/solution.py
@@ -6,6 +6,7 @@
 from jax.experimental import pallas as pl
 from jax.experimental.pallas import tpu as pltpu
 from jax.sharding import PartitionSpec as P
+
 
 LANES = 128
 EPSILON = 1e-06
@@ -70,19 +71,75 @@
     return mixed.astype(jnp.bfloat16).reshape(rows_local, steps_count, out_weight.shape[1])
 
 
-def pack_kernel(q_ref, k_ref, v_ref, g_ref, send_ref):
+def pack_kernel(q_hbm, k_hbm, v_hbm, g_hbm, send_ref, held_ref, sems):
     chips, _, _, width = send_ref.shape
-    rows, steps, _ = q_ref.shape
-    for array, ref in enumerate((q_ref, k_ref, v_ref, g_ref)):
+    _, rows, steps, _ = held_ref.shape
+    copies = [
+        pltpu.make_async_copy(source, held_ref.at[array], sems.at[array])
+        for array, source in enumerate((q_hbm, k_hbm, v_hbm, g_hbm))
+    ]
+    for copy in copies:
+        copy.start()
+    for array, copy in enumerate(copies):
+        copy.wait()
         for chip in range(chips):
             window = slice(chip * width, (chip + 1) * width)
             for row in range(rows):
-                send_ref[chip, array, row * steps : (row + 1) * steps, :] = ref[row, :, window]
+                send_ref[chip, array, row * steps : (row + 1) * steps, :] = held_ref[
+                    array, row, :, window
+                ]
+
+
+def prepare_kernel(
+    rows, steps, heads_here, rate_hbm, size_hbm, _, gain_hbm, state_hbm, state_ref, gain_ref, mix_ref,
+    lead_ref, owner_ref, rate_ref, size_ref, sems,
+):
+    heads, count, _ = mix_ref.shape
+    head = lead_ref.shape[2]
+    prompts = size_hbm.shape[0]
+    device = lax.axis_index("replica")
+    chip = device // CORES
+    core = lax.rem(device, CORES)
+    copies = [
+        pltpu.make_async_copy(source, target, sems.at[number])
+        for number, (source, target) in enumerate(
+            (
+                (rate_hbm, rate_ref),
+                (size_hbm, size_ref),
+                (state_hbm, state_ref),
+                (gain_hbm, gain_ref),
+            )
+        )
+    ]
+    for copy in copies:
+        copy.start()
+    left = lax.broadcasted_iota(jnp.int32, (count, count), 0)
+    right = lax.broadcasted_iota(jnp.int32, (count, count), 1)
+    joined = (left // steps == right // steps) & (left >= right)
+    gap = jnp.maximum(left - right, 0).astype(jnp.float32)
+    index = lax.broadcasted_iota(jnp.int32, (count, head), 0)
+    time = (index % steps + 1).astype(jnp.float32)
+    per_chip = rows * steps
+    row = (index // per_chip * CORES + core) * rows + index % per_chip // steps
+    for copy in copies:
+        copy.wait()
+    owner = jnp.zeros((count, head), jnp.int32)
+    end = jnp.int32(0)
+    for prompt in range(prompts):
+        end = end + size_ref[prompt]
+        owner += (row >= end).astype(jnp.int32)
+    owner_ref[...] = owner
+    for number in range(heads):
+        slot, part = divmod(number, heads_here)
+        place = core if slot == 0 else CORES - 1 - core
+        rate = rate_ref[(chip * CORES + place) * heads_here + part]
+        mix_ref[number] = jnp.where(joined, jnp.exp(-gap * rate), 0.0)
+        lead_ref[number] = jnp.exp(-time * rate)
 
 
 def head_kernel(
-    rows, steps, rate_ref, size_ref, recv_ref, gain_ref, own_state, other_state, own_weight,
-    other_weight, part_ref, hidden_ref, weight_ref, sems,
+    recv_ref, gain_ref, mix_ref, lead_ref, owner_ref, own_state, other_state, own_hbm, other_weight,
+    part_ref, hidden_ref, own_weight, sem,
 ):
     chips, _, per_chip, _ = recv_ref.shape
     count = chips * per_chip
@@ -91,31 +148,15 @@
     device = lax.axis_index("replica")
     chip = device // CORES
     core = lax.rem(device, CORES)
-    copies = [
-        pltpu.make_async_copy(source, weight_ref.at[slot * share : (slot + 1) * share], sems.at[slot])
-        for slot, source in enumerate((own_weight, other_weight))
-    ]
-    for copy in copies:
-        copy.start()
-    index = lax.broadcasted_iota(jnp.int32, (count, head), 0)
-    row = (index // per_chip * CORES + core) * rows + index % per_chip // steps
-    time = (index % steps + 1).astype(jnp.float32)
-    here = []
-    first = jnp.int32(0)
-    for prompt in range(prompts):
-        last = first + size_ref[prompt]
-        here.append((row >= first) & (row < last))
-        first = last
-    left = lax.broadcasted_iota(jnp.int32, (count, count), 0)
-    right = lax.broadcasted_iota(jnp.int32, (count, count), 1)
-    joined = (left // steps == right // steps) & (left >= right)
-    gap = jnp.maximum(left - right, 0).astype(jnp.float32)
+    fetch = pltpu.make_async_copy(own_hbm, own_weight, sem)
+    fetch.start()
+    owner = owner_ref[...]
+    here = [owner == prompt for prompt in range(prompts)]
     squares = jnp.zeros((count, head), jnp.float32)
     for slot, state in enumerate((own_state, other_state)):
         place = core if slot == 0 else CORES - 1 - core
         for part in range(heads_here):
             number = (chip * CORES + place) * heads_here + part
-            rate = rate_ref[number]
             window = pl.ds(pl.multiple_of(place * share + part * head, head), head)
             query, key, value, gate = (
                 recv_ref[:, array, :, window].astype(jnp.float32).reshape(count, head)
@@ -132,14 +173,14 @@
                 (((1,), (1,)), ((), ())),
                 preferred_element_type=jnp.float32,
             )
-            scores = jnp.where(joined, scores * jnp.exp(-gap * rate), 0.0)
+            scores = scores * mix_ref[slot * heads_here + part]
             high = scores.astype(jnp.bfloat16)
             rest = scores - high.astype(jnp.float32)
             low = rest.astype(jnp.bfloat16)
             value = value.astype(jnp.bfloat16)
             recent = jnp.dot(high, value, preferred_element_type=jnp.float32)
             recent += jnp.dot(low, value, preferred_element_type=jnp.float32)
-            attention = jnp.exp(-time * rate) * read + recent
+            attention = lead_ref[slot * heads_here + part] * read + recent
             squares += attention * attention
             scaled = attention * gain_ref[pl.ds(number, 1), :] * jax.nn.sigmoid(gate)
             column = slot * share + part * head
@@ -152,12 +193,16 @@
     tail = jnp.where(lane == 0, high, jnp.where(lane == 1, middle, jnp.where(lane == 2, low, 0.0)))
     width = own_weight.shape[1]
     part_ref[:, :, width:] = tail.reshape(chips, per_chip, LANES).astype(part_ref.dtype)
-    for copy in copies:
-        copy.wait()
+    fetch.wait()
     tile = 512 if width % 512 == 0 else LANES
     for start in range(0, width, tile):
         columns = slice(start, start + tile)
-        block = jnp.dot(hidden_ref[...], weight_ref[:, columns], preferred_element_type=jnp.float32)
+        block = jnp.dot(
+            hidden_ref[:, :share], own_weight[:, columns], preferred_element_type=jnp.float32
+        )
+        block += jnp.dot(
+            hidden_ref[:, share:], other_weight[:, columns], preferred_element_type=jnp.float32
+        )
         part_ref[:, :, columns] = block.reshape(chips, per_chip, tile).astype(part_ref.dtype)
 
 
@@ -178,24 +223,40 @@
 ):
     replicas = lax.axis_size("replica")
     rows, steps, features = queries.shape
-    prompts, share, head = prompt_states.shape
+    _, share, head = prompt_states.shape
     width = out_weight.shape[1]
     chips = replicas // CORES
     per_chip = rows * steps
     wide = share * CORES
     swap = [(i, i + 1 - 2 * (i % CORES)) for i in range(replicas)]
     peers = [[i * CORES + core for i in range(chips)] for core in range(CORES)]
-    other_state = lax.ppermute(prompt_states, "replica", swap)
-    other_weight = lax.ppermute(out_weight, "replica", swap)
+    queries, keys, values, gate_input, decay_rate, group_sizes, gains, near_state, near_weight = (
+        pltpu.with_memory_space_constraint(array, pltpu.HBM)
+        for array in (
+            queries,
+            keys,
+            values,
+            gate_input,
+            decay_rate,
+            group_sizes,
+            norm_gain.reshape(features // head, head),
+            prompt_states,
+            out_weight,
+        )
+    )
     vmem = pl.BlockSpec(memory_space=pltpu.VMEM)
     smem = pl.BlockSpec(memory_space=pltpu.SMEM)
-    whole = pl.BlockSpec(memory_space=pl.ANY)
+    far = pl.BlockSpec(memory_space=pltpu.HBM)
     limit = pltpu.CompilerParams(vmem_limit_bytes=24 << 20)
     sent = pl.pallas_call(
         pack_kernel,
         out_shape=jax.ShapeDtypeStruct((chips, 4, per_chip, wide), queries.dtype),
-        in_specs=[vmem] * 4,
+        in_specs=[far] * 4,
         out_specs=vmem,
+        scratch_shapes=[
+            pltpu.VMEM((4, rows, steps, features), queries.dtype),
+            pltpu.SemaphoreType.DMA((4,)),
+        ],
         compiler_params=limit,
         name="pack",
     )(queries, keys, values, gate_input)
@@ -208,28 +269,42 @@
         axis_index_groups=peers,
     )
     held = exchange(sent)
+    other_state = lax.ppermute(prompt_states, "replica", swap)
+    other_weight = lax.ppermute(out_weight, "replica", swap)
+    count = chips * per_chip
+    heads = wide // head
+    state, gain, mix, lead, owner = pl.pallas_call(
+        functools.partial(prepare_kernel, rows, steps, share // head),
+        out_shape=(
+            jax.ShapeDtypeStruct(prompt_states.shape, prompt_states.dtype),
+            jax.ShapeDtypeStruct((features // head, head), jnp.float32),
+            jax.ShapeDtypeStruct((heads, count, count), jnp.float32),
+            jax.ShapeDtypeStruct((heads, count, head), jnp.float32),
+            jax.ShapeDtypeStruct((count, head), jnp.int32),
+        ),
+        in_specs=[far] * 5,
+        out_specs=(vmem,) * 5,
+        scratch_shapes=[
+            pltpu.SMEM(decay_rate.shape, decay_rate.dtype),
+            pltpu.SMEM(group_sizes.shape, group_sizes.dtype),
+            pltpu.SemaphoreType.DMA((4,)),
+        ],
+        compiler_params=limit,
+        name="prepare",
+    )(decay_rate, group_sizes, sent, gains, near_state)
     parts = pl.pallas_call(
-        functools.partial(head_kernel, rows, steps),
+        head_kernel,
         out_shape=jax.ShapeDtypeStruct((chips, per_chip, width + LANES), jnp.bfloat16),
-        in_specs=[smem, smem, vmem, vmem, vmem, vmem, whole, whole],
+        in_specs=[vmem] * 7 + [far, vmem],
         out_specs=vmem,
         scratch_shapes=[
-            pltpu.VMEM((chips * per_chip, wide), jnp.bfloat16),
-            pltpu.VMEM((wide, width), out_weight.dtype),
-            pltpu.SemaphoreType.DMA((2,)),
+            pltpu.VMEM((count, wide), jnp.bfloat16),
+            pltpu.VMEM(out_weight.shape, out_weight.dtype),
+            pltpu.SemaphoreType.DMA(()),
         ],
         compiler_params=limit,
         name="heads",
-    )(
-        decay_rate,
-        group_sizes,
-        held,
-        norm_gain.reshape(features // head, head),
-        prompt_states,
-        other_state,
-        out_weight,
-        other_weight,
-    )
+    )(held, gain, mix, lead, owner, state, other_state, near_weight, other_weight)
     returned = exchange(parts)
     return pl.pallas_call(
         functools.partial(finish_kernel, features),

time: 44.7 us -> 38.2 us (0.85)
  local copies, waits for them, and re-layouts: 7.74 us -> 0 us
  Pallas kernels: 3.61 us -> 6.1 us
  waiting for transfers between devices: 9.36 us -> 8.31 us
    unnamed x18 -> x0, local copies, waits for them, and re-layouts: 7.74 us -> none
    pallas_call x1 -> x2, Pallas kernels: 2.11 us -> 3.7 us  [the longest x1 2.65 us: whole_plan(): pl.pallas_call(head_kernel, out_shape=jax.ShapeDtypeStruct((chips, per_ch...]
    ppermute x1, waiting for transfers between devices: 1.52 us -> 0.47 us  [whole_plan(): other_state = lax.ppermute(prompt_states, 'replica', swap)]
    pallas_call x1, Pallas kernels: 0.77 us -> 1.67 us  [whole_plan(): pl.pallas_call(pack_kernel, out_shape=jax.ShapeDtypeStruct((chips, 4, per...]
  transfers between devices with their start and end apart: 3 -> 3, of which waited for: 2 -> 2; matrix products, arithmetic and copies ran while one was open for 0% -> 0% of each run, Pallas kernels for 2% -> 7%
where the time goes in v2:
time: 38.2 us; the launch traced here: 37.9 us
  blocking collectives  15.9 us (42%)
  waiting for transfers between devices  8.31 us (22%)
  starting transfers between devices  7.52 us (20%)
  Pallas kernels  6.1 us (16%)
    all_to_all x1, blocking collectives, whole_plan(): returned = exchange(parts)  15.9 us
    all_to_all x1, waiting for transfers between devices, whole_plan(): held = exchange(sent)  7.84 us
    all_to_all x1, starting transfers between devices, whole_plan(): held = exchange(sent)  6.8 us
    pallas_call x1, Pallas kernels, whole_plan(): pl.pallas_call(head_kernel, out_shape=jax.ShapeDtypeStruct((chips, per_ch...  2.65 us
    pallas_call x1, Pallas kernels, whole_plan(): pl.pallas_call(pack_kernel, out_shape=jax.ShapeDtypeStruct((chips, 4, per...  1.67 us
    pallas_call x1, Pallas kernels, whole_plan(): pl.pallas_call(functools.partial(prepare_kernel, rows, steps, share // he...  1.04 us
  transfers between devices with their start and end apart: 3, of which 2 were waited for; matrix products, arithmetic and copies ran while one was open for 0% of the time, Pallas kernels for 7%

profile of v2, /device:TPU:0, one launch (start us, length us, event | category | flops | bytes accessed | tf_op | source)
XLA Modules:
  0.0 37.9 jit_solution(15130504279009846914)
XLA Ops:
  0.0 0.5 %collective-permute-start.1 = (bf16[256,3072]{1,0:T(8,128)(2,1)}, bf16[256,3072]{1,0:T(8,128)(2,1)S(1)}, u32[]{:S(2)}, u32[]{:S(2)}) collective-permute-start(bf16[256,3072]{1,0:T(8,128)(2,1)} %own_hbm.1), channel_id=1, source_target_pairs={{0,1},{1,0},{2,3},{3,2},{4,5},{5,4},{6,7},{7,6},{8,9},{9,8},{10,11... | collective-permute-start | bytes 4718600 | tf_op jit(solution)/shard_map/ppermute | solution.py:273
  0.5 1.7 %pack.1._ = bf16[8,4,8,512]{3,2,1,0:T(8,128)(2,1)} custom-call(bf16[2,4,4096]{2,1,0:T(4,128)(2,1)} %q_hbm.1, bf16[2,4,4096]{2,1,0:T(4,128)(2,1)} %k_hbm.1, bf16[2,4,4096]{2,1,0:T(4,128)(2,1)} %v_hbm.1, bf16[2,4,4096]{2,1,0:T(4,128)(2,1)} %g_hbm.1), custom_call_target="tpu_custom_call" | custom-call | tf_op jit(solution)/shard_map/pack/pallas_call | solution.py:251
  2.2 6.8 %all-to-all-start = ((bf16[8,4,8,512]{3,2,1,0:T(8,128)(2,1)}), bf16[8,4,8,512]{3,2,1,0:T(8,128)(2,1)S(1)}, u32[]{:S(2)}, u32[]{:S(2)}) async-start(bf16[8,4,8,512]{3,2,1,0:T(8,128)(2,1)} %pack.1._), calls=%async_computation | async-start | bytes 524288 | tf_op jit(solution)/shard_map/all_to_all | solution.py:271
  9.0 0.2 collective-permute-start
  9.2 1.0 %prepare.1 = (bf16[4,256,128]{2,1,0:T(8,128)(2,1)S(1)}, f32[32,128]{1,0:T(8,128)S(1)}, f32[4,64,64]{2,1,0:T(8,128)S(1)}, f32[4,64,128]{2,1,0:T(8,128)S(1)}, s32[64,128]{1,0:T(8,128)S(1)}) custom-call(f32[32]{0:T(128)} %rate_hbm.1, s32[4]{0:T(128)} %size_hbm.1, bf16[8,4,8,512]{3,2,1,0:T(8,128)(2,1)} %pack.1._, f32[32,128]{1,0:T(8,128)} %bitcast.1, ...), custom_call_target="tpu_custom_call" | custom-call | tf_op jit(solution)/shard_map/prepare/pallas_call | solution.py:276
  10.3 0.5 %collective-permute-done.other_state = bf16[4,256,128]{2,1,0:T(8,128)(2,1)S(1)} collective-permute-done((bf16[4,256,128]{2,1,0:T(8,128)(2,1)}, bf16[4,256,128]{2,1,0:T(8,128)(2,1)S(1)}, u32[]{:S(2)}, u32[]{:S(2)}) %collective-permute-start) | collective-permute-done | bytes 262176 | tf_op jit(solution)/shard_map/ppermute | solution.py:272
  10.7 7.8 %all-to-all-done.recv_ref = bf16[8,4,8,512]{3,2,1,0:T(8,128)(2,1)S(1)} async-done(((bf16[8,4,8,512]{3,2,1,0:T(8,128)(2,1)}), bf16[8,4,8,512]{3,2,1,0:T(8,128)(2,1)S(1)}, u32[]{:S(2)}, u32[]{:S(2)}) %all-to-all-start) | async-done | bytes 262176 | tf_op jit(solution)/shard_map/all_to_all | solution.py:271
  18.6 0.0 collective-permute-done.1.other_weight
  18.6 2.7 %heads.1 = bf16[8,8,3200]{2,1,0:T(8,128)(2,1)S(1)} custom-call(bf16[8,4,8,512]{3,2,1,0:T(8,128)(2,1)S(1)} %all-to-all-done.recv_ref, f32[32,128]{1,0:T(8,128)S(1)} %get-tuple-element.10.gain_ref, f32[4,64,64]{2,1,0:T(8,128)S(1)} %get-tuple-element.11.mix_ref, f32[4,64,128]{2,1,0:T(8,128)S(1)} %get-tuple-element.12.lead_ref, ...), custom_call_target="tpu_custom_call" | custom-call | tf_op jit(solution)/shard_map/heads/pallas_call | solution.py:295
  21.2 15.9 %all_to_all.10.part_ref = bf16[8,8,3200]{2,1,0:T(8,128)(2,1)S(1)} all-to-all(bf16[8,8,3200]{2,1,0:T(8,128)(2,1)S(1)} %heads.1), channel_id=1, replica_groups={{0,2,4,6,8,10,12,14},{1,3,5,7,9,11,13,15},{16,18,20,22,24,26,28,30},{17..., dimensions={0} | all-to-all | bytes 819200 | tf_op jit(solution)/shard_map/all_to_all | solution.py:308
  37.2 0.7 %finish.1 = bf16[2,4,3072]{2,1,0:T(4,128)(2,1)} custom-call(bf16[8,8,3200]{2,1,0:T(8,128)(2,1)S(1)} %all_to_all.10.part_ref), custom_call_target="tpu_custom_call" | custom-call | tf_op jit(solution)/shard_map/finish/pallas_call | solution.py:309
Async XLA Ops:
  0.0 18.6 %collective-permute-start.1 = (bf16[256,3072]{1,0:T(8,128)(2,1)}, bf16[256,3072]{1,0:T(8,128)(2,1)S(1)}, u32[]{:S(2)}, u32[]{:S(2)}) collective-permute-start(bf16[256,3072]{1,0:T(8,128)(2,1)} %own_hbm.1), channel_id=1, source_target_pairs={{0,1},{1,0},{2,3},{3,2},{4,5},{5,4},{6,7},{7,6},{8,9},{9,8},{10,11... | collective-permute-start | bytes 4718600 | tf_op jit(solution)/shard_map/ppermute | solution.py:273
  2.2 16.4 %all-to-all-start = ((bf16[8,4,8,512]{3,2,1,0:T(8,128)(2,1)}), bf16[8,4,8,512]{3,2,1,0:T(8,128)(2,1)S(1)}, u32[]{:S(2)}, u32[]{:S(2)}) async-start(bf16[8,4,8,512]{3,2,1,0:T(8,128)(2,1)} %pack.1._), calls=%async_computation | async-start | bytes 524288 | tf_op jit(solution)/shard_map/all_to_all | solution.py:271
  9.0 1.7 %collective-permute-start = (bf16[4,256,128]{2,1,0:T(8,128)(2,1)}, bf16[4,256,128]{2,1,0:T(8,128)(2,1)S(1)}, u32[]{:S(2)}, u32[]{:S(2)}) collective-permute-start(bf16[4,256,128]{2,1,0:T(8,128)(2,1)} %state_hbm.1), channel_id=1, source_target_pairs={{0,1},{1,0},{2,3},{3,2},{4,5},{5,4},{6,7},{7,6},{8,9},{9,8},{10,11... | collective-permute-start | bytes 786440 | tf_op jit(solution)/shard_map/ppermute | solution.py:272
